TPU v7x, 256 devices: a whole 4x4x8 slice. The times are simulated.
256 devices in a mesh: rows: 32 (over z, x), feat: 8 (over y, core).
Axes of the slice: x: 4, y: 4, z: 8, core: 2. Of those that a mesh axis runs over, the one named last changes fastest.
Arguments:
- points: float32 [8, 131072], P(None, 'rows'), may hold values from -4 to 4
- freq_index: int32 [8, 16384], P(None, 'feat'), may hold values from -12 to 12
- log_density: float32 [16384], P('feat'), may hold values from -3 to 2.7
- targets: float32 [131072], P('rows'), may hold values from -16 to 16
- probes: int32 [31, 131072], P(None, 'rows'), may hold values 0 or 1
Outputs:
- solution: float32 [32, 131072], P(None, 'rows')
- residual: float32 [32, 131072], P(None, 'rows')
All inputs are finite; a program needn't handle non-finite values. No bound on the sum of `probes` on one device may be relied on, other than what follows from the above.
Results may differ from a plain program's by a relative error of at most 0.0025.
Values may be sent and summed in bfloat16 or wider, within the bound.
A program may use at most 128 MiB of HBM per device.

v0:
```python
import math
import jax
import jax.numpy as jnp
from jax import lax
from jax.sharding import PartitionSpec as P

FREQS = 16384
ITERS = 2
frequency_step = 0.25
noise_level = 1.0


def build_features(points, frequency, amplitude, block_rows):
    rows_here = points.shape[1]
    blocks = rows_here // block_rows
    feature_width = 2 * frequency.shape[1]

    def fill(block_index, table):
        first_row = (block_index * block_rows).astype(jnp.int32)
        point_block = lax.dynamic_slice_in_dim(points, first_row, block_rows, 1)
        phases = jnp.dot(
            point_block.T,
            frequency,
            precision=lax.Precision.HIGHEST,
            preferred_element_type=jnp.float32,
        )
        block = jnp.concatenate(
            [amplitude * jnp.cos(phases), amplitude * jnp.sin(phases)], axis=1
        ).astype(jnp.bfloat16)
        return lax.dynamic_update_slice_in_dim(table, block, first_row, 0)

    initial = jnp.zeros((rows_here, feature_width), jnp.bfloat16)
    return lax.fori_loop(0, blocks, fill, initial)


def squared_norm(values):
    return lax.psum(jnp.sum(values * values, axis=1), "rows")


def local(points, freq_index, log_density, targets, probes):
    rows_here = points.shape[1]
    block_rows = math.gcd(rows_here, 512)
    frequency = frequency_step * freq_index.astype(jnp.float32)
    amplitude = jnp.exp(0.5 * log_density) / math.sqrt(FREQS)
    features = build_features(points, frequency, amplitude, block_rows)
    right_sides = jnp.concatenate([targets[None, :], (2 * probes - 1).astype(jnp.float32)], axis=0)
    solution = jnp.zeros_like(right_sides)
    residual = right_sides
    direction = right_sides
    residual_energy = squared_norm(right_sides)
    for iteration in range(ITERS):
        direction_bf = direction.astype(jnp.bfloat16)
        partial_coeffs = jnp.dot(direction_bf, features, preferred_element_type=jnp.float32)
        coeff_bf = lax.psum(partial_coeffs, "rows").astype(jnp.bfloat16)
        coeff_bf = lax.optimization_barrier(coeff_bf)
        partial_images = lax.dot_general(
            coeff_bf, features, (((1,), (1,)), ((), ())), preferred_element_type=jnp.float32
        )
        coeff_wide = coeff_bf.astype(jnp.float32)
        energy_part = jnp.sum(coeff_wide * coeff_wide, axis=1)
        images = lax.psum(partial_images, "feat")
        feature_energy = lax.psum(energy_part, "feat")
        direction_energy = lax.psum(jnp.sum(direction * direction, axis=1), "rows")
        curvature = feature_energy + noise_level * direction_energy
        step_size = residual_energy / curvature
        solution = solution + step_size[:, None] * direction
        residual = residual - step_size[:, None] * (images + noise_level * direction)
        if iteration + 1 < ITERS:
            energy_next = squared_norm(residual)
            mixing = energy_next / residual_energy
            direction = residual + mixing[:, None] * direction
            residual_energy = energy_next
    return (solution, residual)


def solution(mesh):
    in_specs = (P(None, "rows"), P(None, "feat"), P("feat"), P("rows"), P(None, "rows"))
    out_specs = (P(None, "rows"), P(None, "rows"))
    return jax.shard_map(local, mesh=mesh, in_specs=in_specs, out_specs=out_specs, check_vma=False)
```

profile of v0, /device:TPU:2, one launch (start us, length us, event | category | flops | bytes accessed | tf_op | source)
XLA Modules:
  0.0 764.3 jit_solution(17343094420450126333)
XLA Ops:
  7.2 0.0 all-reduce.7.cloned.1.call-start
  7.2 0.7 exponential_multiply_fusion
  7.9 0.8 convert_multiply_fusion
  8.8 11.0 %broadcast_in_dim.9 = bf16[4096,4096]{1,0:T(8,128)(2,1)} broadcast(bf16[]{:T(256)} %constant.42.clone.1), dimensions={} | broadcast | bytes 33554432 | tf_op jit(solution)/shard_map/broadcast_in_dim | solution.py:32
  19.7 0.0 copy-start.2
  19.7 0.0 copy-start.1
  19.7 182.7 %while.13 = (s32[]{:T(128)}, bf16[4096,4096]{1,0:T(8,128)(2,1)}, f32[2048]{0:T(1024)S(1)}, f32[8,4096]{1,0:T(8,128)}, f32[8,2048]{1,0:T(8,128)S(1)}, /*index=5*/s32[]{:T(128)}, s32[]{:T(128)}, s32[]{:T(128)}, s32[]{:T(128)}) while((s32[]{:T(128)}, bf16[4096,4096]{1,0:T(8,128)(2,1)}, f32[2048]{0:T(1024)S(1)}, f32[8,4096]{1,0:T(8,128)}, ...), condition=%wide.region_3.0_spmd, body=%wide.region_2.0_spmd.sunk | while | flops 113246216 | bytes 12673179 | solution.py:33
  19.7 20.4 %multiply_convert_fusion.3 = (bf16[512,2048]{1,0:T(8,128)(2,1)S(1)}, bf16[512,2048]{1,0:T(8,128)(2,1)S(1)}) fusion(f32[2048]{0:T(1024)S(1)} %get-tuple-element.170, f32[8,2048]{1,0:T(8,128)S(1)} %get-tuple-element.172, f32[8,4096]{1,0:T(8,128)} %get-tuple-element.171, s32[]{:T(128)S(6)} %select_n.9), kind=kOutput, calls=%fused_computation.2.clone.1 | convolution fusion | flops 104857600 | bytes 4284420 | tf_op jit(solution)/shard_map/while/body/eval_jaxpr/dot_general | solution.py:21
  40.2 2.4 maximum_dynamic-update-slice_fusion.2
  42.6 20.4 %multiply_convert_fusion.3 = (bf16[512,2048]{1,0:T(8,128)(2,1)S(1)}, bf16[512,2048]{1,0:T(8,128)(2,1)S(1)}) fusion(f32[2048]{0:T(1024)S(1)} %get-tuple-element.170, f32[8,2048]{1,0:T(8,128)S(1)} %get-tuple-element.172, f32[8,4096]{1,0:T(8,128)} %get-tuple-element.171, s32[]{:T(128)S(6)} %select_n.9), kind=kOutput, calls=%fused_computation.2.clone.1 | convolution fusion | flops 104857600 | bytes 4284420 | tf_op jit(solution)/shard_map/while/body/eval_jaxpr/dot_general | solution.py:21
  63.0 2.5 maximum_dynamic-update-slice_fusion.2
  65.4 20.4 %multiply_convert_fusion.3 = (bf16[512,2048]{1,0:T(8,128)(2,1)S(1)}, bf16[512,2048]{1,0:T(8,128)(2,1)S(1)}) fusion(f32[2048]{0:T(1024)S(1)} %get-tuple-element.170, f32[8,2048]{1,0:T(8,128)S(1)} %get-tuple-element.172, f32[8,4096]{1,0:T(8,128)} %get-tuple-element.171, s32[]{:T(128)S(6)} %select_n.9), kind=kOutput, calls=%fused_computation.2.clone.1 | convolution fusion | flops 104857600 | bytes 4284420 | tf_op jit(solution)/shard_map/while/body/eval_jaxpr/dot_general | solution.py:21
  85.8 2.5 maximum_dynamic-update-slice_fusion.2
  88.3 20.4 %multiply_convert_fusion.3 = (bf16[512,2048]{1,0:T(8,128)(2,1)S(1)}, bf16[512,2048]{1,0:T(8,128)(2,1)S(1)}) fusion(f32[2048]{0:T(1024)S(1)} %get-tuple-element.170, f32[8,2048]{1,0:T(8,128)S(1)} %get-tuple-element.172, f32[8,4096]{1,0:T(8,128)} %get-tuple-element.171, s32[]{:T(128)S(6)} %select_n.9), kind=kOutput, calls=%fused_computation.2.clone.1 | convolution fusion | flops 104857600 | bytes 4284420 | tf_op jit(solution)/shard_map/while/body/eval_jaxpr/dot_general | solution.py:21
  108.7 2.5 maximum_dynamic-update-slice_fusion.2
  111.1 20.4 %multiply_convert_fusion.3 = (bf16[512,2048]{1,0:T(8,128)(2,1)S(1)}, bf16[512,2048]{1,0:T(8,128)(2,1)S(1)}) fusion(f32[2048]{0:T(1024)S(1)} %get-tuple-element.170, f32[8,2048]{1,0:T(8,128)S(1)} %get-tuple-element.172, f32[8,4096]{1,0:T(8,128)} %get-tuple-element.171, s32[]{:T(128)S(6)} %select_n.9), kind=kOutput, calls=%fused_computation.2.clone.1 | convolution fusion | flops 104857600 | bytes 4284420 | tf_op jit(solution)/shard_map/while/body/eval_jaxpr/dot_general | solution.py:21
  131.5 2.4 maximum_dynamic-update-slice_fusion.2
  133.9 20.4 %multiply_convert_fusion.3 = (bf16[512,2048]{1,0:T(8,128)(2,1)S(1)}, bf16[512,2048]{1,0:T(8,128)(2,1)S(1)}) fusion(f32[2048]{0:T(1024)S(1)} %get-tuple-element.170, f32[8,2048]{1,0:T(8,128)S(1)} %get-tuple-element.172, f32[8,4096]{1,0:T(8,128)} %get-tuple-element.171, s32[]{:T(128)S(6)} %select_n.9), kind=kOutput, calls=%fused_computation.2.clone.1 | convolution fusion | flops 104857600 | bytes 4284420 | tf_op jit(solution)/shard_map/while/body/eval_jaxpr/dot_general | solution.py:21
  154.3 2.5 maximum_dynamic-update-slice_fusion.2
  156.8 20.4 %multiply_convert_fusion.3 = (bf16[512,2048]{1,0:T(8,128)(2,1)S(1)}, bf16[512,2048]{1,0:T(8,128)(2,1)S(1)}) fusion(f32[2048]{0:T(1024)S(1)} %get-tuple-element.170, f32[8,2048]{1,0:T(8,128)S(1)} %get-tuple-element.172, f32[8,4096]{1,0:T(8,128)} %get-tuple-element.171, s32[]{:T(128)S(6)} %select_n.9), kind=kOutput, calls=%fused_computation.2.clone.1 | convolution fusion | flops 104857600 | bytes 4284420 | tf_op jit(solution)/shard_map/while/body/eval_jaxpr/dot_general | solution.py:21
  177.2 2.5 maximum_dynamic-update-slice_fusion.2
  179.6 20.4 %multiply_convert_fusion.3 = (bf16[512,2048]{1,0:T(8,128)(2,1)S(1)}, bf16[512,2048]{1,0:T(8,128)(2,1)S(1)}) fusion(f32[2048]{0:T(1024)S(1)} %get-tuple-element.170, f32[8,2048]{1,0:T(8,128)S(1)} %get-tuple-element.172, f32[8,4096]{1,0:T(8,128)} %get-tuple-element.171, s32[]{:T(128)S(6)} %select_n.9), kind=kOutput, calls=%fused_computation.2.clone.1 | convolution fusion | flops 104857600 | bytes 4284420 | tf_op jit(solution)/shard_map/while/body/eval_jaxpr/dot_general | solution.py:21
  200.0 2.4 maximum_dynamic-update-slice_fusion.2
  202.5 0.0 copy-done.2
  202.5 0.1 add_convert_fusion
  202.5 0.0 copy-done.1
  202.5 0.2 multiply_reduce_fusion.4
  202.7 13.5 %fusion.5 = f32[32,4096]{1,0:T(8,128)S(1)} fusion(bf16[4096,4096]{1,0:T(8,128)(2,1)} %get-tuple-element.96, f32[31,4096]{1,0:T(8,128)S(1)} %add_convert_fusion, f32[1,4096]{1,0:T(1,128)S(1)} %bitcast.11), kind=kOutput, calls=%fused_computation.19 | convolution fusion | flops 1074266112 | bytes 34603008 | tf_op jit(solution)/shard_map/dot_general | solution.py:53
  216.3 146.9 %all-reduce.10 = (bf16[32,4096]{1,0:T(8,128)(2,1)S(1)}, f32[32]{0:T(128)S(1)}) all-reduce(f32[32,4096]{1,0:T(8,128)S(1)} %fusion.5, f32[32]{0:T(128)S(1)} %multiply_reduce_fusion.4), channel_id=1, replica_groups=mesh['rows'=32,'feat'=8] {'rows'}, use_global_device_ids=true, to_apply=%region_4.0 | all-reduce | flops 131104 | bytes 786688 | tf_op jit(solution)/shard_map/psum | solution.py:54
  363.2 16.0 %fusion.8 = f32[32,4096]{1,0:T(8,128)} fusion(bf16[32,4096]{1,0:T(8,128)(2,1)S(1)} %get-tuple-element.109, bf16[4096,4096]{1,0:T(8,128)(2,1)} %get-tuple-element.96), kind=kOutput, calls=%fused_computation.26 | convolution fusion | flops 1073741824 | bytes 34340864 | tf_op jit(solution)/shard_map/dot_general | solution.py:56
  379.2 0.0 all-reduce.7.cloned.1.call-update
  379.2 0.0 all-reduce.9.cloned.1.call-start
  379.3 0.2 multiply_reduce_fusion.3
  379.5 12.4 %psum.68 = f32[32]{0:T(128)S(1)} all-reduce(f32[32]{0:T(128)S(1)} %multiply_reduce_fusion.3), channel_id=1, replica_groups=mesh['rows'=32,'feat'=8] {'feat'}, use_global_device_ids=true, to_apply=%region_6.0 | all-reduce | flops 32 | bytes 256 | tf_op jit(solution)/shard_map/psum | solution.py:62
  391.9 53.1 %all-reduce.7.cloned.1.call-done = f32[32,4096]{1,0:T(8,128)} async-done(((f32[32,4096]{1,0:T(8,128)}), f32[32,4096]{1,0:T(8,128)}) %all-reduce.7.cloned.1.call-update) | async-done | bytes 524304 | tf_op jit(solution)/shard_map/psum | solution.py:61
  445.0 0.0 copy-start
  445.0 1.4 multiply_reduce_fusion.2
  446.4 71.1 %psum.70 = f32[32]{0:T(128)S(1)} all-reduce(f32[32]{0:T(128)S(1)} %multiply_reduce_fusion.2), channel_id=1, replica_groups=mesh['rows'=32,'feat'=8] {'rows'}, use_global_device_ids=true, to_apply=%region_9.0 | all-reduce | flops 32 | bytes 256 | tf_op jit(solution)/shard_map/psum | solution.py:37
  517.5 13.8 %fusion.3 = f32[32,4096]{1,0:T(8,128)S(1)} fusion(bf16[4096,4096]{1,0:T(8,128)(2,1)} %get-tuple-element.96, f32[32]{0:T(128)S(1)} %div.18, f32[31,4096]{1,0:T(8,128)S(1)} %add_convert_fusion, f32[1,4096]{1,0:T(1,128)S(1)} %bitcast.13, f32[32,4096]{1,0:T(8,128)} %all-reduce.7.cloned.1.call-done, f32[32]{0:T(128)S(1)} %add_divide_fusion), kind=kOutput, calls=%fused_computation.17 | convolution fusion | flops 1074659328 | bytes 35127552 | tf_op jit(solution)/shard_map/dot_general | solution.py:53
  531.3 0.0 copy-done
  531.3 0.3 multiply_reduce_fusion
  531.6 145.0 %all-reduce.11 = (bf16[32,4096]{1,0:T(8,128)(2,1)S(1)}, f32[32]{0:T(128)S(1)}) all-reduce(f32[32,4096]{1,0:T(8,128)S(1)} %fusion.3, f32[32]{0:T(128)S(1)} %multiply_reduce_fusion), channel_id=1, replica_groups=mesh['rows'=32,'feat'=8] {'rows'}, use_global_device_ids=true, to_apply=%region_10.0 | all-reduce | flops 131104 | bytes 786688 | tf_op jit(solution)/shard_map/psum | solution.py:54
  676.6 16.0 %fusion.9 = f32[32,4096]{1,0:T(8,128)} fusion(bf16[32,4096]{1,0:T(8,128)(2,1)S(1)} %get-tuple-element.107, bf16[4096,4096]{1,0:T(8,128)(2,1)} %get-tuple-element.96), kind=kOutput, calls=%fused_computation.27 | convolution fusion | flops 1073741824 | bytes 34340864 | tf_op jit(solution)/shard_map/dot_general | solution.py:56
  692.6 0.0 all-reduce.9.cloned.1.call-update
  692.6 0.2 multiply_reduce_fusion.1
  692.8 12.4 %psum.72 = f32[32]{0:T(128)S(1)} all-reduce(f32[32]{0:T(128)S(1)} %multiply_reduce_fusion.1), channel_id=1, replica_groups=mesh['rows'=32,'feat'=8] {'feat'}, use_global_device_ids=true, to_apply=%region_12.0 | all-reduce | flops 32 | bytes 256 | tf_op jit(solution)/shard_map/psum | solution.py:62
  705.2 49.9 %all-reduce.9.cloned.1.call-done = f32[32,4096]{1,0:T(8,128)} async-done(((f32[32,4096]{1,0:T(8,128)}), f32[32,4096]{1,0:T(8,128)}) %all-reduce.9.cloned.1.call-update) | async-done | bytes 524304 | tf_op jit(solution)/shard_map/psum | solution.py:61
  755.1 2.3 multiply_subtract_fusion
  (3 shorter events, 0.0 us)
Async XLA Ops:
  7.2 437.9 %all-reduce.7.cloned.1.call-start = ((), (), s32[]{:S(2)}) async-start(), calls=%async_computation | async-start | bytes 1048576 | tf_op jit(solution)/shard_map/psum | solution.py:61
  19.7 182.7 %copy-start.2 = (s32[31,4096]{1,0:T(8,128)S(1)}, s32[31,4096]{1,0:T(8,128)}, u32[]{:S(2)}) copy-start(s32[31,4096]{1,0:T(8,128)} %param.11) | copy-start | bytes 1523716
  19.7 182.8 %copy-start.1 = (f32[4096]{0:T(1024)S(1)}, f32[4096]{0:T(1024)}, u32[]{:S(2)}) copy-start(f32[4096]{0:T(1024)} %param.10) | copy-start | bytes 49156
  379.2 375.9 %all-reduce.9.cloned.1.call-start = ((), (), s32[]{:S(2)}) async-start(), calls=%async_computation.1 | async-start | bytes 1048576 | tf_op jit(solution)/shard_map/psum | solution.py:61
  445.0 86.3 %copy-start = (f32[32,4096]{1,0:T(8,128)S(1)}, f32[32,4096]{1,0:T(8,128)}, u32[]{:S(2)}) copy-start(f32[32,4096]{1,0:T(8,128)} %all-reduce.7.cloned.1.call-done) | copy-start | bytes 1572868
Sparse Core Ops, SparseCore 0:
  379.4 65.6 all-reduce.6
  692.7 62.3 all-reduce.8
where the time goes:
time: 765 us; the launch traced here: 764 us
  blocking collectives  388 us (51%)
  matrix products  222 us (29%)
  waiting for transfers between devices  103 us (13%)
  other arithmetic  25.8 us (3%)
  between operations  14.1 us (2%)
  local copies, waits for them, and re-layouts  11 us (1%)
    psum x2, blocking collectives, local(): coeff_bf = lax.psum(partial_coeffs, 'rows').astype(jnp.bfloat16)  292 us
    dot_general x8, matrix products, fill(): jnp.dot(point_block.T, frequency, precision=lax.Precision.HIGHEST, prefer...  163 us
    psum x2, waiting for transfers between devices, local(): images = lax.psum(partial_images, 'feat')  103 us
    psum x1, blocking collectives, squared_norm(): return lax.psum(jnp.sum(values * values, axis=1), 'rows')  71.1 us
    dot_general x2, matrix products, local(): lax.dot_general(coeff_bf, features, (((1,), (1,)), ((), ())), preferred_e...  32 us
    dot_general x2, matrix products, local(): jnp.dot(direction_bf, features, preferred_element_type=jnp.float32)  27.3 us
    psum x2, blocking collectives, local(): feature_energy = lax.psum(energy_part, 'feat')  24.8 us
    dynamic_update_slice x8, other arithmetic, fill(): return lax.dynamic_update_slice_in_dim(table, block, first_row, 0)  19.7 us
  transfers between devices with their start and end apart: 2, of which 2 were waited for; matrix products, arithmetic and copies ran while one was open for 0% of the time, Pallas kernels for 0%

commit v1 on v0

--- a/solution.py
+++ b/solution.py
@@ -58,7 +58,9 @@
         )
         coeff_wide = coeff_bf.astype(jnp.float32)
         energy_part = jnp.sum(coeff_wide * coeff_wide, axis=1)
-        images = lax.psum(partial_images, "feat")
+        images = partial_images
+        for hop in (1, 2, 4):
+            images = images + lax.ppermute(images, "feat", [(dev, dev ^ hop) for dev in range(8)])
         feature_energy = lax.psum(energy_part, "feat")
         direction_energy = lax.psum(jnp.sum(direction * direction, axis=1), "rows")
         curvature = feature_energy + noise_level * direction_energy

time: 765 us -> 698 us (0.912)
  waiting for transfers between devices: 103 us -> 28.9 us
  between operations: 14.1 us -> 0.71 us
  blocking collectives: 388 us -> 399 us
  starting transfers between devices: 0.08 us -> 7.93 us
    psum x2 -> x0, waiting for transfers between devices: 103 us -> none  [local(): images = lax.psum(partial_images, 'feat')]
    ppermute x0 -> x6, waiting for transfers between devices: none -> 28.9 us  [local(): lax.ppermute(images, 'feat', [(dev, dev ^ hop) for dev in range(8)])]
    psum x2, blocking collectives: 24.8 us -> 36.6 us  [local(): feature_energy = lax.psum(energy_part, 'feat')]
    ppermute x0 -> x6, starting transfers between devices: none -> 7.93 us  [local(): lax.ppermute(images, 'feat', [(dev, dev ^ hop) for dev in range(8)])]
  transfers between devices with their start and end apart: 2 -> 6, of which waited for: 2 -> 4; matrix products, arithmetic and copies ran while one was open for 0% -> 0% of each run, Pallas kernels for 0% -> 0%
where the time goes in v1:
time: 698 us; the launch traced here: 693 us
  blocking collectives  399 us (57%)
  matrix products  221 us (32%)
  waiting for transfers between devices  28.9 us (4%)
  other arithmetic  24 us (3%)
  local copies, waits for them, and re-layouts  11 us (2%)
  starting transfers between devices  7.93 us (1%)
    psum x2, blocking collectives, local(): coeff_bf = lax.psum(partial_coeffs, 'rows').astype(jnp.bfloat16)  287 us
    dot_general x8, matrix products, fill(): jnp.dot(point_block.T, frequency, precision=lax.Precision.HIGHEST, prefer...  163 us
    psum x1, blocking collectives, squared_norm(): return lax.psum(jnp.sum(values * values, axis=1), 'rows')  75.4 us
    psum x2, blocking collectives, local(): feature_energy = lax.psum(energy_part, 'feat')  36.6 us
    dot_general x2, matrix products, local(): lax.dot_general(coeff_bf, features, (((1,), (1,)), ((), ())), preferred_e...  30.6 us
    ppermute x6, waiting for transfers between devices, local(): lax.ppermute(images, 'feat', [(dev, dev ^ hop) for dev in range(8)])  28.9 us
    dot_general x2, matrix products, local(): jnp.dot(direction_bf, features, preferred_element_type=jnp.float32)  27.1 us
    dynamic_update_slice x8, other arithmetic, fill(): return lax.dynamic_update_slice_in_dim(table, block, first_row, 0)  19.7 us
  transfers between devices with their start and end apart: 6, of which 4 were waited for; matrix products, arithmetic and copies ran while one was open for 0% of the time, Pallas kernels for 0%

profile of v1, /device:TPU:2, one launch (start us, length us, event | category | flops | bytes accessed | tf_op | source)
XLA Modules:
  0.0 692.7 jit_solution(5797195477211097075)
XLA Ops:
  0.6 0.7 exponential_multiply_fusion
  1.3 0.8 convert_multiply_fusion
  2.2 11.0 %broadcast_in_dim.9 = bf16[4096,4096]{1,0:T(8,128)(2,1)} broadcast(bf16[]{:T(256)} %constant.42.clone.1), dimensions={} | broadcast | bytes 33554432 | tf_op jit(solution)/shard_map/broadcast_in_dim | solution.py:32
  13.2 182.7 %while.13 = (s32[]{:T(128)}, bf16[4096,4096]{1,0:T(8,128)(2,1)}, f32[2048]{0:T(1024)S(1)}, f32[8,4096]{1,0:T(8,128)}, f32[8,2048]{1,0:T(8,128)S(1)}, /*index=5*/s32[]{:T(128)}, s32[]{:T(128)}, s32[]{:T(128)}, s32[]{:T(128)}) while((s32[]{:T(128)}, bf16[4096,4096]{1,0:T(8,128)(2,1)}, f32[2048]{0:T(1024)S(1)}, f32[8,4096]{1,0:T(8,128)}, ...), condition=%wide.region_3.0_spmd, body=%wide.region_2.0_spmd.sunk | while | flops 113246216 | bytes 12673179 | solution.py:33
  13.2 20.4 %multiply_convert_fusion.3 = (bf16[512,2048]{1,0:T(8,128)(2,1)S(1)}, bf16[512,2048]{1,0:T(8,128)(2,1)S(1)}) fusion(f32[2048]{0:T(1024)S(1)} %get-tuple-element.172, f32[8,2048]{1,0:T(8,128)S(1)} %get-tuple-element.174, f32[8,4096]{1,0:T(8,128)} %get-tuple-element.173, s32[]{:T(128)S(6)} %select_n.9), kind=kOutput, calls=%fused_computation.2.clone.1 | convolution fusion | flops 104857600 | bytes 4284420 | tf_op jit(solution)/shard_map/while/body/eval_jaxpr/dot_general | solution.py:21
  33.6 2.4 maximum_dynamic-update-slice_fusion.2
  36.0 20.4 %multiply_convert_fusion.3 = (bf16[512,2048]{1,0:T(8,128)(2,1)S(1)}, bf16[512,2048]{1,0:T(8,128)(2,1)S(1)}) fusion(f32[2048]{0:T(1024)S(1)} %get-tuple-element.172, f32[8,2048]{1,0:T(8,128)S(1)} %get-tuple-element.174, f32[8,4096]{1,0:T(8,128)} %get-tuple-element.173, s32[]{:T(128)S(6)} %select_n.9), kind=kOutput, calls=%fused_computation.2.clone.1 | convolution fusion | flops 104857600 | bytes 4284420 | tf_op jit(solution)/shard_map/while/body/eval_jaxpr/dot_general | solution.py:21
  56.4 2.5 maximum_dynamic-update-slice_fusion.2
  58.9 20.4 %multiply_convert_fusion.3 = (bf16[512,2048]{1,0:T(8,128)(2,1)S(1)}, bf16[512,2048]{1,0:T(8,128)(2,1)S(1)}) fusion(f32[2048]{0:T(1024)S(1)} %get-tuple-element.172, f32[8,2048]{1,0:T(8,128)S(1)} %get-tuple-element.174, f32[8,4096]{1,0:T(8,128)} %get-tuple-element.173, s32[]{:T(128)S(6)} %select_n.9), kind=kOutput, calls=%fused_computation.2.clone.1 | convolution fusion | flops 104857600 | bytes 4284420 | tf_op jit(solution)/shard_map/while/body/eval_jaxpr/dot_general | solution.py:21
  79.2 2.5 maximum_dynamic-update-slice_fusion.2
  81.7 20.4 %multiply_convert_fusion.3 = (bf16[512,2048]{1,0:T(8,128)(2,1)S(1)}, bf16[512,2048]{1,0:T(8,128)(2,1)S(1)}) fusion(f32[2048]{0:T(1024)S(1)} %get-tuple-element.172, f32[8,2048]{1,0:T(8,128)S(1)} %get-tuple-element.174, f32[8,4096]{1,0:T(8,128)} %get-tuple-element.173, s32[]{:T(128)S(6)} %select_n.9), kind=kOutput, calls=%fused_computation.2.clone.1 | convolution fusion | flops 104857600 | bytes 4284420 | tf_op jit(solution)/shard_map/while/body/eval_jaxpr/dot_general | solution.py:21
  102.1 2.5 maximum_dynamic-update-slice_fusion.2
  104.6 20.4 %multiply_convert_fusion.3 = (bf16[512,2048]{1,0:T(8,128)(2,1)S(1)}, bf16[512,2048]{1,0:T(8,128)(2,1)S(1)}) fusion(f32[2048]{0:T(1024)S(1)} %get-tuple-element.172, f32[8,2048]{1,0:T(8,128)S(1)} %get-tuple-element.174, f32[8,4096]{1,0:T(8,128)} %get-tuple-element.173, s32[]{:T(128)S(6)} %select_n.9), kind=kOutput, calls=%fused_computation.2.clone.1 | convolution fusion | flops 104857600 | bytes 4284420 | tf_op jit(solution)/shard_map/while/body/eval_jaxpr/dot_general | solution.py:21
  124.9 2.4 maximum_dynamic-update-slice_fusion.2
  127.4 20.4 %multiply_convert_fusion.3 = (bf16[512,2048]{1,0:T(8,128)(2,1)S(1)}, bf16[512,2048]{1,0:T(8,128)(2,1)S(1)}) fusion(f32[2048]{0:T(1024)S(1)} %get-tuple-element.172, f32[8,2048]{1,0:T(8,128)S(1)} %get-tuple-element.174, f32[8,4096]{1,0:T(8,128)} %get-tuple-element.173, s32[]{:T(128)S(6)} %select_n.9), kind=kOutput, calls=%fused_computation.2.clone.1 | convolution fusion | flops 104857600 | bytes 4284420 | tf_op jit(solution)/shard_map/while/body/eval_jaxpr/dot_general | solution.py:21
  147.7 2.5 maximum_dynamic-update-slice_fusion.2
  150.2 20.4 %multiply_convert_fusion.3 = (bf16[512,2048]{1,0:T(8,128)(2,1)S(1)}, bf16[512,2048]{1,0:T(8,128)(2,1)S(1)}) fusion(f32[2048]{0:T(1024)S(1)} %get-tuple-element.172, f32[8,2048]{1,0:T(8,128)S(1)} %get-tuple-element.174, f32[8,4096]{1,0:T(8,128)} %get-tuple-element.173, s32[]{:T(128)S(6)} %select_n.9), kind=kOutput, calls=%fused_computation.2.clone.1 | convolution fusion | flops 104857600 | bytes 4284420 | tf_op jit(solution)/shard_map/while/body/eval_jaxpr/dot_general | solution.py:21
  170.6 2.5 maximum_dynamic-update-slice_fusion.2
  173.1 20.4 %multiply_convert_fusion.3 = (bf16[512,2048]{1,0:T(8,128)(2,1)S(1)}, bf16[512,2048]{1,0:T(8,128)(2,1)S(1)}) fusion(f32[2048]{0:T(1024)S(1)} %get-tuple-element.172, f32[8,2048]{1,0:T(8,128)S(1)} %get-tuple-element.174, f32[8,4096]{1,0:T(8,128)} %get-tuple-element.173, s32[]{:T(128)S(6)} %select_n.9), kind=kOutput, calls=%fused_computation.2.clone.1 | convolution fusion | flops 104857600 | bytes 4284420 | tf_op jit(solution)/shard_map/while/body/eval_jaxpr/dot_general | solution.py:21
  193.4 2.4 maximum_dynamic-update-slice_fusion.2
  196.0 0.2 multiply_reduce_fusion.4
  196.2 13.5 %fusion.5 = f32[32,4096]{1,0:T(8,128)S(1)} fusion(bf16[4096,4096]{1,0:T(8,128)(2,1)} %get-tuple-element.96, f32[31,4096]{1,0:T(8,128)S(1)} %add_convert_fusion, f32[1,4096]{1,0:T(1,128)S(1)} %bitcast.11), kind=kOutput, calls=%fused_computation.19 | convolution fusion | flops 1074266112 | bytes 34603008 | tf_op jit(solution)/shard_map/dot_general | solution.py:53
  209.7 146.9 %all-reduce.4 = (bf16[32,4096]{1,0:T(8,128)(2,1)S(1)}, f32[32]{0:T(128)S(1)}) all-reduce(f32[32,4096]{1,0:T(8,128)S(1)} %fusion.5, f32[32]{0:T(128)S(1)} %multiply_reduce_fusion.4), channel_id=1, replica_groups=mesh['rows'=32,'feat'=8] {'rows'}, use_global_device_ids=true, to_apply=%region_4.0 | all-reduce | flops 131104 | bytes 786688 | tf_op jit(solution)/shard_map/psum | solution.py:54
  356.6 15.3 %fusion.8 = f32[32,4096]{1,0:T(8,128)S(1)} fusion(bf16[32,4096]{1,0:T(8,128)(2,1)S(1)} %get-tuple-element.109, bf16[4096,4096]{1,0:T(8,128)(2,1)} %get-tuple-element.96), kind=kOutput, calls=%fused_computation.26 | convolution fusion | flops 1073741824 | bytes 34340864 | tf_op jit(solution)/shard_map/dot_general | solution.py:56
  371.9 0.1 collective-permute-start
  372.0 1.9 collective-permute-done
  373.9 0.1 add.77
  374.0 1.7 collective-permute-start.1
  375.7 12.4 %collective-permute-done.1 = f32[32,4096]{1,0:T(8,128)S(1)} collective-permute-done((f32[32,4096]{1,0:T(8,128)S(1)}, f32[32,4096]{1,0:T(8,128)S(1)}, u32[]{:S(2)}, u32[]{:S(2)}) %collective-permute-start.1) | collective-permute-done | bytes 524320 | tf_op jit(solution)/shard_map/ppermute | solution.py:63
  388.1 0.1 add.78
  388.2 3.3 collective-permute-start.2
  391.4 0.2 multiply_reduce_fusion.3
  391.6 18.1 %psum.54 = f32[32]{0:T(128)S(1)} all-reduce(f32[32]{0:T(128)S(1)} %multiply_reduce_fusion.3), channel_id=1, replica_groups=mesh['rows'=32,'feat'=8] {'feat'}, use_global_device_ids=true, to_apply=%region_6.0 | all-reduce | flops 32 | bytes 256 | tf_op jit(solution)/shard_map/psum | solution.py:64
  409.7 0.3 multiply_reduce_fusion.2
  410.0 75.4 %psum.55 = f32[32]{0:T(128)S(1)} all-reduce(f32[32]{0:T(128)S(1)} %get-tuple-element.111), channel_id=1, replica_groups=mesh['rows'=32,'feat'=8] {'rows'}, use_global_device_ids=true, to_apply=%region_8.0 | all-reduce | flops 32 | bytes 256 | tf_op jit(solution)/shard_map/psum | solution.py:37
  485.4 13.6 %fusion.3 = f32[32,4096]{1,0:T(8,128)S(1)} fusion(bf16[4096,4096]{1,0:T(8,128)(2,1)} %get-tuple-element.96, f32[32,4096]{1,0:T(8,128)S(1)} %get-tuple-element.112, f32[32]{0:T(128)S(1)} %div.18, f32[31,4096]{1,0:T(8,128)S(1)} %add_convert_fusion, f32[1,4096]{1,0:T(1,128)S(1)} %bitcast.13), kind=kOutput, calls=%fused_computation.17 | convolution fusion | flops 1074266112 | bytes 35127424 | tf_op jit(solution)/shard_map/dot_general | solution.py:53
  499.0 0.3 multiply_reduce_fusion
  499.3 140.5 %all-reduce.5 = (bf16[32,4096]{1,0:T(8,128)(2,1)S(1)}, f32[32]{0:T(128)S(1)}) all-reduce(f32[32,4096]{1,0:T(8,128)S(1)} %fusion.3, f32[32]{0:T(128)S(1)} %multiply_reduce_fusion), channel_id=1, replica_groups=mesh['rows'=32,'feat'=8] {'rows'}, use_global_device_ids=true, to_apply=%region_9.0 | all-reduce | flops 131104 | bytes 786688 | tf_op jit(solution)/shard_map/psum | solution.py:54
  639.7 15.3 %fusion.9 = f32[32,4096]{1,0:T(8,128)S(1)} fusion(bf16[32,4096]{1,0:T(8,128)(2,1)S(1)} %get-tuple-element.107, bf16[4096,4096]{1,0:T(8,128)(2,1)} %get-tuple-element.96), kind=kOutput, calls=%fused_computation.27 | convolution fusion | flops 1073741824 | bytes 34340864 | tf_op jit(solution)/shard_map/dot_general | solution.py:56
  655.1 0.1 collective-permute-start.3
  655.2 1.9 collective-permute-done.3
  657.1 0.1 add.84
  657.1 1.3 collective-permute-start.4
  658.5 12.7 %collective-permute-done.4 = f32[32,4096]{1,0:T(8,128)S(1)} collective-permute-done((f32[32,4096]{1,0:T(8,128)S(1)}, f32[32,4096]{1,0:T(8,128)S(1)}, u32[]{:S(2)}, u32[]{:S(2)}) %collective-permute-start.4) | collective-permute-done | bytes 524320 | tf_op jit(solution)/shard_map/ppermute | solution.py:63
  671.3 1.5 collective-permute-start.5
  672.8 0.2 multiply_reduce_fusion.1
  672.9 18.5 %psum.57 = f32[32]{0:T(128)S(1)} all-reduce(f32[32]{0:T(128)S(1)} %multiply_reduce_fusion.1), channel_id=1, replica_groups=mesh['rows'=32,'feat'=8] {'feat'}, use_global_device_ids=true, to_apply=%region_11.0 | all-reduce | flops 32 | bytes 256 | tf_op jit(solution)/shard_map/psum | solution.py:64
  691.5 1.2 multiply_subtract_fusion
  (11 shorter events, 0.1 us)
Async XLA Ops:
  13.1 182.7 %copy-start.1 = (s32[31,4096]{1,0:T(8,128)S(1)}, s32[31,4096]{1,0:T(8,128)}, u32[]{:S(2)}) copy-start(s32[31,4096]{1,0:T(8,128)} %param.11) | copy-start | bytes 1523716
  13.1 182.8 %copy-start = (f32[4096]{0:T(1024)S(1)}, f32[4096]{0:T(1024)}, u32[]{:S(2)}) copy-start(f32[4096]{0:T(1024)} %param.10) | copy-start | bytes 49156
  371.9 2.0 collective-permute-start
  374.0 14.1 %collective-permute-start.1 = (f32[32,4096]{1,0:T(8,128)S(1)}, f32[32,4096]{1,0:T(8,128)S(1)}, u32[]{:S(2)}, u32[]{:S(2)}) collective-permute-start(f32[32,4096]{1,0:T(8,128)S(1)} %add.77), channel_id=1, source_target_pairs={{0,2},{1,3},{2,0},{3,1},{4,6},{5,7},{6,4},{7,5},{8,10},{9,11},{10,... | collective-permute-start | bytes 1572872 | tf_op jit(solution)/shard_map/ppermute | solution.py:63
  388.2 21.5 %collective-permute-start.2 = (f32[32,4096]{1,0:T(8,128)S(1)}, f32[32,4096]{1,0:T(8,128)S(1)}, u32[]{:S(2)}, u32[]{:S(2)}) collective-permute-start(f32[32,4096]{1,0:T(8,128)S(1)} %add.78), channel_id=1, source_target_pairs={{0,4},{1,5},{2,6},{3,7},{4,0},{5,1},{6,2},{7,3},{8,12},{9,13},{10,... | collective-permute-start | bytes 1572872 | tf_op jit(solution)/shard_map/ppermute | solution.py:63
  655.1 2.0 collective-permute-start.3
  657.1 14.1 %collective-permute-start.4 = (f32[32,4096]{1,0:T(8,128)S(1)}, f32[32,4096]{1,0:T(8,128)S(1)}, u32[]{:S(2)}, u32[]{:S(2)}) collective-permute-start(f32[32,4096]{1,0:T(8,128)S(1)} %add.84), channel_id=1, source_target_pairs={{0,2},{1,3},{2,0},{3,1},{4,6},{5,7},{6,4},{7,5},{8,10},{9,11},{10,... | collective-permute-start | bytes 1572872 | tf_op jit(solution)/shard_map/ppermute | solution.py:63
  671.3 20.2 %collective-permute-start.5 = (f32[32,4096]{1,0:T(8,128)S(1)}, f32[32,4096]{1,0:T(8,128)S(1)}, u32[]{:S(2)}, u32[]{:S(2)}) collective-permute-start(f32[32,4096]{1,0:T(8,128)S(1)} %add.85), channel_id=1, source_target_pairs={{0,4},{1,5},{2,6},{3,7},{4,0},{5,1},{6,2},{7,3},{8,12},{9,13},{10,... | collective-permute-start | bytes 1572872 | tf_op jit(solution)/shard_map/ppermute | solution.py:63
